TPU v7x, 512 devices: a whole 4x8x8 slice. The times are simulated.
512 devices in a mesh: segment: 4 (over x), graph: 128 (over y, z, core).
Axes of the slice: x: 4, y: 8, z: 8, core: 2. Of those that a mesh axis runs over, the one named last changes fastest.
Arguments:
- features: bfloat16 [65536, 1024], P('graph'), may hold values from -6 to 6
- weights: bfloat16 [8, 1024, 1024], P(None, 'graph'), may hold values from -0.75 to 0.75
- history: bfloat16 [8, 8192, 1024], P(None, 'graph'), may hold values from 0 to 1.1953125
- own_adj: bfloat16 [4, 16384, 128], P(None, 'graph'), may hold values from 0 to 0.00390625
- side_adj: bfloat16 [4, 4, 2048, 128], P(None, None, 'graph'), may hold values from 0 to 0.012451172
- hist_adj: bfloat16 [4, 8192, 128], P(None, 'graph'), may hold values from 0 to 0.009338379
- send_ids: int32 [4, 4, 2048], P(None, None, 'graph'), may hold values from 0 to 127, as said below
- hist_ids: int32 [4, 8192], P(None, 'graph'), may hold values from 0 to 63
Outputs:
- layer_out: bfloat16 [8, 65536, 1024], P('segment', 'graph')
Inputs may be any that keep to these rules, and one draw needn't show every extreme that they name: `send_ids`: each list of 16 row numbers for one batch, one partition and one direction has distinct entries.
All inputs are finite; a program needn't handle non-finite values.
Results may differ from a plain program's by a relative error of at most 0.0032.
Values may be sent and summed in bfloat16 or wider, within the bound.
No kernel may reach another device: no remote copies, remote signals or barrier semaphores. Data moves between devices by JAX's collectives and lax.ppermute only.
A program may use at most 64 MiB of HBM per device.

v0:
```python
import jax
import jax.numpy as jnp
from jax import lax
from jax.sharding import PartitionSpec as P

ALPHA = 0.1
LAMBDA = 1.5
BF = jnp.bfloat16
F32 = jnp.float32


def dot(a, b):
    return jnp.dot(a, b, preferred_element_type=F32)


def dot_t(a, b):
    return lax.dot_general(a, b, (((0,), (0,)), ((), ())), preferred_element_type=F32)


def one_hot(ids, width):
    return (ids[:, None] == lax.broadcasted_iota(jnp.int32, (ids.shape[0], width), 1)).astype(BF)


def shards(features, weights, history, own_adj, side_adj, hist_adj, send_ids, hist_ids):
    segment_pos = lax.axis_index("segment")
    segment_count = lax.axis_size("segment")
    graph_count = lax.axis_size("graph")
    core = lax.axis_index("graph") % 2
    chip_odd = lax.axis_index("graph") // 2 % 2
    layers, _, width = weights.shape
    rows = own_adj.shape[2]
    edge = send_ids.shape[2]
    kept = layers // segment_count
    resident = lax.all_gather(weights, "graph", axis=1, tiled=True)

    def partner(value):
        return lax.ppermute(value, "graph", [(p, p ^ 1) for p in range(graph_count)])

    def exchange(value, first):
        pairs = []
        for p in range(first, graph_count - first - 2, 4):
            for c in range(2):
                pairs += [(p + c, p + c + 2), (p + c + 2, p + c)]
        return lax.ppermute(value, "graph", pairs)

    def pick_batch(value):
        return lax.dynamic_index_in_dim(value, segment_pos, 0, keepdims=False)

    def by_part(mine, theirs):
        return (jnp.where(core == 0, mine, theirs), jnp.where(core == 0, theirs, mine))

    initial = lax.dynamic_slice_in_dim(features, segment_pos * rows, rows, 0)
    own = pick_batch(own_adj)
    side = pick_batch(side_adj).reshape(4 * edge, rows)
    hist = pick_batch(hist_adj)
    sids = pick_batch(send_ids).reshape(-1)
    hids = pick_batch(hist_ids)
    tables = jnp.concatenate([own, side, hist], axis=0)
    ids = jnp.concatenate([sids, hids])
    i0, i1 = by_part(ids, partner(ids))
    t0, t1 = by_part(tables, partner(tables))
    x0, x1 = by_part(initial, partner(initial))
    looked = jax.vmap(lambda t: dot(one_hot(hids, t.shape[0]), t).astype(BF))(history)
    g0, g1 = by_part(looked, partner(looked))

    def split(t, i):
        own = t[:rows]
        side = [t[rows + k * edge : rows + (k + 1) * edge] for k in range(4)]
        hist = t[rows + 4 * edge :]
        send = [one_hot(i[k * edge : (k + 1) * edge], rows) for k in range(4)]
        return (own, side, hist, send)

    own0, side0, hist0, send0 = split(t0, i0)
    own1, side1, hist1, send1 = split(t1, i1)
    q10 = dot_t(side1[0], send0[0]).astype(BF)
    q01 = dot_t(side0[1], send1[1]).astype(BF)
    near = jnp.concatenate(
        [jnp.concatenate([own0, q01], axis=1), jnp.concatenate([q10, own1], axis=1)], axis=0
    )
    zs = jnp.zeros_like(side0[0])
    from_before = jnp.concatenate(
        [
            jnp.concatenate([side0[0], side0[2], zs], axis=0),
            jnp.concatenate([zs, zs, side1[2]], axis=0),
        ],
        axis=1,
    )
    from_after = jnp.concatenate(
        [
            jnp.concatenate([side0[3], zs, zs], axis=0),
            jnp.concatenate([zs, side1[1], side1[3]], axis=0),
        ],
        axis=1,
    )
    to_after = jnp.concatenate(
        [
            jnp.concatenate([zs, send1[0]], axis=1),
            jnp.concatenate([send0[2], zs], axis=1),
            jnp.concatenate([zs, send1[2]], axis=1),
        ],
        axis=0,
    )
    to_before = jnp.concatenate(
        [
            jnp.concatenate([send0[3], zs], axis=1),
            jnp.concatenate([send0[1], zs], axis=1),
            jnp.concatenate([zs, send1[3]], axis=1),
        ],
        axis=0,
    )
    far_a = jnp.where(chip_odd == 0, from_after, from_before)
    far_b = jnp.where(chip_odd == 0, from_before, from_after)
    pick_a = jnp.where(chip_odd == 0, to_after, to_before)
    pick_b = jnp.where(chip_odd == 0, to_before, to_after)
    zh = jnp.zeros_like(hist0)
    hist_t = jnp.concatenate(
        [jnp.concatenate([hist0, zh], axis=1), jnp.concatenate([zh, hist1], axis=1)], axis=0
    )
    looked = jnp.concatenate([g0, g1], axis=1)
    start = jnp.concatenate([x0, x1], axis=0)
    current = start
    own_rows = []
    for layer in range(layers):
        strength = jnp.log(jnp.float32(LAMBDA / (layer + 1.0)) + 1.0)
        got_a = exchange(dot(pick_a, current).astype(BF), 0)
        got_b = exchange(dot(pick_b, current).astype(BF), 2)
        local = dot(near, current) + dot_t(hist_t, looked[layer])
        total = local + dot_t(far_a, got_a) + dot_t(far_b, got_b)
        support = (1.0 - ALPHA) * total + ALPHA * start.astype(F32)
        mixing = dot(support.astype(BF), resident[layer])
        current = jax.nn.relu((1.0 - strength) * support + strength * mixing).astype(BF)
        own_rows.append(lax.dynamic_slice_in_dim(current, core * rows, rows, 0))
    whole = jnp.stack(own_rows).reshape(segment_count, kept, rows, width)
    exchanged = lax.all_to_all(whole, "segment", 0, 0)
    return exchanged.transpose(1, 0, 2, 3).reshape(kept, segment_count * rows, width)


def solution(mesh):
    in_specs = (
        P("graph", None),
        P(None, "graph", None),
        P(None, "graph", None),
        P(None, "graph", None),
        P(None, None, "graph", None),
        P(None, "graph", None),
        P(None, None, "graph"),
        P(None, "graph"),
    )
    out_specs = P("segment", "graph", None)
    return jax.shard_map(shards, mesh=mesh, in_specs=in_specs, out_specs=out_specs, check_vma=False)
```

profile of v0, /device:TPU:32, one launch (start us, length us, event | category | flops | bytes accessed | tf_op | source)
XLA Modules:
  0.0 252.8 jit_solution(157648303293373457)
XLA Ops:
  11.7 2.4 collective-permute-start.2
  16.8 1.9 collective-permute-start
  19.2 2.4 collective-permute-start.3
  25.1 10.8 %collective-permute-start.5 = (bf16[48,1024]{1,0:T(8,128)(2,1)S(1)}, bf16[48,1024]{1,0:T(8,128)(2,1)S(1)}, u32[]{:S(2)}, u32[]{:S(2)}) collective-permute-start(bf16[48,1024]{1,0:T(8,128)(2,1)S(1)} %convolution_convert_fusion.15), channel_id=1, source_target_pairs={{2,4},{4,2},{3,5},{5,3},{6,8},{8,6},{7,9},{9,7},{10,12},{12,10},{1... | collective-permute-start | bytes 294920 | tf_op jit(solution)/shard_map/ppermute | solution.py:44
  36.1 1.9 collective-permute-start.4
  39.4 3.6 %collective-permute-done.4 = bf16[48,1024]{1,0:T(8,128)(2,1)S(1)} collective-permute-done((bf16[48,1024]{1,0:T(8,128)(2,1)S(1)}, bf16[48,1024]{1,0:T(8,128)(2,1)S(1)}, u32[]{:S(2)}, u32[]{:S(2)}) %collective-permute-start.4) | collective-permute-done | bytes 98336 | tf_op jit(solution)/shard_map/ppermute | solution.py:44
  46.5 68.9 %all-gather.2.cloned.1.call-done = bf16[8,1024,1024]{2,1,0:T(8,128)(2,1)} async-done(((bf16[8,8,1024]{2,1,0:T(8,128)(2,1)}), bf16[8,1024,1024]{2,1,0:T(8,128)(2,1)}) %all-gather.2.cloned.1.call-update) | async-done | bytes 16777232 | tf_op jit(solution)/shard_map/all_gather | solution.py:34
  115.3 3.1 %maximum_convert_fusion.6 = bf16[256,1024]{1,0:T(8,128)(2,1)S(1)} fusion(f32[256,1024]{1,0:T(8,128)} %fusion.19, bf16[8,1024,1024]{2,1,0:T(8,128)(2,1)} %all-gather.2.cloned.1.call-done), kind=kOutput, calls=%fused_computation.103 | convolution fusion | flops 538443776 | bytes 4718592 | tf_op jit(solution)/shard_map/dot_general | solution.py:13
  119.2 4.4 %collective-permute-start.7 = (bf16[48,1024]{1,0:T(8,128)(2,1)S(1)}, bf16[48,1024]{1,0:T(8,128)(2,1)S(1)}, u32[]{:S(2)}, u32[]{:S(2)}) collective-permute-start(bf16[48,1024]{1,0:T(8,128)(2,1)S(1)} %convolution_convert_fusion.13), channel_id=1, source_target_pairs={{2,4},{4,2},{3,5},{5,3},{6,8},{8,6},{7,9},{9,7},{10,12},{12,10},{1... | collective-permute-start | bytes 294920 | tf_op jit(solution)/shard_map/ppermute | solution.py:44
  125.8 3.5 %collective-permute-done.7 = bf16[48,1024]{1,0:T(8,128)(2,1)S(1)} collective-permute-done((bf16[48,1024]{1,0:T(8,128)(2,1)S(1)}, bf16[48,1024]{1,0:T(8,128)(2,1)S(1)}, u32[]{:S(2)}, u32[]{:S(2)}) %collective-permute-start.7) | collective-permute-done | bytes 98336 | tf_op jit(solution)/shard_map/ppermute | solution.py:44
  130.8 2.4 maximum_convert_fusion.5
  134.0 4.8 %collective-permute-start.9 = (bf16[48,1024]{1,0:T(8,128)(2,1)S(1)}, bf16[48,1024]{1,0:T(8,128)(2,1)S(1)}, u32[]{:S(2)}, u32[]{:S(2)}) collective-permute-start(bf16[48,1024]{1,0:T(8,128)(2,1)S(1)} %convolution_convert_fusion.11), channel_id=1, source_target_pairs={{2,4},{4,2},{3,5},{5,3},{6,8},{8,6},{7,9},{9,7},{10,12},{12,10},{1... | collective-permute-start | bytes 294920 | tf_op jit(solution)/shard_map/ppermute | solution.py:44
  141.1 2.7 %collective-permute-done.9 = bf16[48,1024]{1,0:T(8,128)(2,1)S(1)} collective-permute-done((bf16[48,1024]{1,0:T(8,128)(2,1)S(1)}, bf16[48,1024]{1,0:T(8,128)(2,1)S(1)}, u32[]{:S(2)}, u32[]{:S(2)}) %collective-permute-start.9) | collective-permute-done | bytes 98336 | tf_op jit(solution)/shard_map/ppermute | solution.py:44
  146.0 2.4 maximum_convert_fusion.4
  149.2 4.3 %collective-permute-start.11 = (bf16[48,1024]{1,0:T(8,128)(2,1)S(1)}, bf16[48,1024]{1,0:T(8,128)(2,1)S(1)}, u32[]{:S(2)}, u32[]{:S(2)}) collective-permute-start(bf16[48,1024]{1,0:T(8,128)(2,1)S(1)} %convolution_convert_fusion.9), channel_id=1, source_target_pairs={{2,4},{4,2},{3,5},{5,3},{6,8},{8,6},{7,9},{9,7},{10,12},{12,10},{1... | collective-permute-start | bytes 294920 | tf_op jit(solution)/shard_map/ppermute | solution.py:44
  155.8 3.2 %collective-permute-done.11 = bf16[48,1024]{1,0:T(8,128)(2,1)S(1)} collective-permute-done((bf16[48,1024]{1,0:T(8,128)(2,1)S(1)}, bf16[48,1024]{1,0:T(8,128)(2,1)S(1)}, u32[]{:S(2)}, u32[]{:S(2)}) %collective-permute-start.11) | collective-permute-done | bytes 98336 | tf_op jit(solution)/shard_map/ppermute | solution.py:44
  160.7 2.4 maximum_convert_fusion.3
  163.9 4.8 %collective-permute-start.13 = (bf16[48,1024]{1,0:T(8,128)(2,1)S(1)}, bf16[48,1024]{1,0:T(8,128)(2,1)S(1)}, u32[]{:S(2)}, u32[]{:S(2)}) collective-permute-start(bf16[48,1024]{1,0:T(8,128)(2,1)S(1)} %convolution_convert_fusion.7), channel_id=1, source_target_pairs={{2,4},{4,2},{3,5},{5,3},{6,8},{8,6},{7,9},{9,7},{10,12},{12,10},{1... | collective-permute-start | bytes 294920 | tf_op jit(solution)/shard_map/ppermute | solution.py:44
  171.0 2.7 %collective-permute-done.13 = bf16[48,1024]{1,0:T(8,128)(2,1)S(1)} collective-permute-done((bf16[48,1024]{1,0:T(8,128)(2,1)S(1)}, bf16[48,1024]{1,0:T(8,128)(2,1)S(1)}, u32[]{:S(2)}, u32[]{:S(2)}) %collective-permute-start.13) | collective-permute-done | bytes 98336 | tf_op jit(solution)/shard_map/ppermute | solution.py:44
  175.9 2.4 maximum_convert_fusion.2
  179.1 4.3 %collective-permute-start.15 = (bf16[48,1024]{1,0:T(8,128)(2,1)S(1)}, bf16[48,1024]{1,0:T(8,128)(2,1)S(1)}, u32[]{:S(2)}, u32[]{:S(2)}) collective-permute-start(bf16[48,1024]{1,0:T(8,128)(2,1)S(1)} %convolution_convert_fusion.5), channel_id=1, source_target_pairs={{2,4},{4,2},{3,5},{5,3},{6,8},{8,6},{7,9},{9,7},{10,12},{12,10},{1... | collective-permute-start | bytes 294920 | tf_op jit(solution)/shard_map/ppermute | solution.py:44
  183.8 2.1 collective-permute-start.14
  185.9 3.0 %collective-permute-done.15 = bf16[48,1024]{1,0:T(8,128)(2,1)S(1)} collective-permute-done((bf16[48,1024]{1,0:T(8,128)(2,1)S(1)}, bf16[48,1024]{1,0:T(8,128)(2,1)S(1)}, u32[]{:S(2)}, u32[]{:S(2)}) %collective-permute-start.15) | collective-permute-done | bytes 98336 | tf_op jit(solution)/shard_map/ppermute | solution.py:44
  190.7 2.4 maximum_convert_fusion.1
  193.8 4.8 %collective-permute-start.17 = (bf16[48,1024]{1,0:T(8,128)(2,1)S(1)}, bf16[48,1024]{1,0:T(8,128)(2,1)S(1)}, u32[]{:S(2)}, u32[]{:S(2)}) collective-permute-start(bf16[48,1024]{1,0:T(8,128)(2,1)S(1)} %convolution_convert_fusion.3), channel_id=1, source_target_pairs={{2,4},{4,2},{3,5},{5,3},{6,8},{8,6},{7,9},{9,7},{10,12},{12,10},{1... | collective-permute-start | bytes 294920 | tf_op jit(solution)/shard_map/ppermute | solution.py:44
  199.0 1.9 collective-permute-start.16
  201.0 2.7 %collective-permute-done.17 = bf16[48,1024]{1,0:T(8,128)(2,1)S(1)} collective-permute-done((bf16[48,1024]{1,0:T(8,128)(2,1)S(1)}, bf16[48,1024]{1,0:T(8,128)(2,1)S(1)}, u32[]{:S(2)}, u32[]{:S(2)}) %collective-permute-start.17) | collective-permute-done | bytes 98336 | tf_op jit(solution)/shard_map/ppermute | solution.py:44
  205.9 2.4 maximum_convert_fusion
  209.1 4.3 %collective-permute-start.19 = (bf16[48,1024]{1,0:T(8,128)(2,1)S(1)}, bf16[48,1024]{1,0:T(8,128)(2,1)S(1)}, u32[]{:S(2)}, u32[]{:S(2)}) collective-permute-start(bf16[48,1024]{1,0:T(8,128)(2,1)S(1)} %convolution_convert_fusion.1), channel_id=1, source_target_pairs={{2,4},{4,2},{3,5},{5,3},{6,8},{8,6},{7,9},{9,7},{10,12},{12,10},{1... | collective-permute-start | bytes 294920 | tf_op jit(solution)/shard_map/ppermute | solution.py:44
  215.7 3.2 %collective-permute-done.19 = bf16[48,1024]{1,0:T(8,128)(2,1)S(1)} collective-permute-done((bf16[48,1024]{1,0:T(8,128)(2,1)S(1)}, bf16[48,1024]{1,0:T(8,128)(2,1)S(1)}, u32[]{:S(2)}, u32[]{:S(2)}) %collective-permute-start.19) | collective-permute-done | bytes 98336 | tf_op jit(solution)/shard_map/ppermute | solution.py:44
  220.6 2.3 fusion
  223.0 21.4 %all_to_all.5 = bf16[4,2,128,1024]{3,2,1,0:T(8,128)(2,1)S(1)} all-to-all(bf16[4,2,128,1024]{3,2,1,0:T(8,128)(2,1)S(1)} %bitcast.146), channel_id=1, replica_groups=mesh['segment'=4,'graph'=128] {'segment'}, dimensions={0} | all-to-all | bytes 4194304 | tf_op jit(solution)/shard_map/all_to_all | solution.py:134
  (123 shorter events, 48.3 us)
Async XLA Ops:
  6.5 12.2 %copy-start = (bf16[8,64,1024]{2,1,0:T(8,128)(2,1)S(1)}, bf16[8,64,1024]{2,1,0:T(8,128)(2,1)}, u32[]{:S(2)}) copy-start(bf16[8,64,1024]{2,1,0:T(8,128)(2,1)} %param.10) | copy-start | bytes 3145732
  6.5 108.8 %all-gather.2.cloned.1.call-start = ((), (), s32[]{:S(2)}) async-start(), calls=%async_computation.1 | async-start | bytes 16908288 | tf_op jit(solution)/shard_map/all_gather | solution.py:34
  8.8 12.9 %collective-permute-start.1 = (s32[128]{0:T(128)S(1)}, s32[128]{0:T(128)S(1)}, u32[]{:S(2)}, u32[]{:S(2)}) collective-permute-start(s32[128]{0:T(128)S(1)} %pad_add_fusion.4), channel_id=1, source_target_pairs={{0,1},{1,0},{2,3},{3,2},{4,5},{5,4},{6,7},{7,6},{8,9},{9,8},{10,11... | collective-permute-start | bytes 1544 | tf_op jit(solution)/shard_map/ppermute | solution.py:37
  11.7 12.1 %collective-permute-start.2 = (bf16[128,1024]{1,0:T(8,128)(2,1)S(1)}, bf16[128,1024]{1,0:T(8,128)(2,1)S(1)}, u32[]{:S(2)}, u32[]{:S(2)}) collective-permute-start(bf16[128,1024]{1,0:T(8,128)(2,1)S(1)} %constant_dynamic-slice_fusion), channel_id=1, source_target_pairs={{0,1},{1,0},{2,3},{3,2},{4,5},{5,4},{6,7},{7,6},{8,9},{9,8},{10,11... | collective-permute-start | bytes 786440 | tf_op jit(solution)/shard_map/ppermute | solution.py:37
  16.8 5.5 %collective-permute-start = (bf16[256,128]{0,1:T(8,128)(2,1)S(1)}, bf16[256,128]{0,1:T(8,128)(2,1)S(1)}, u32[]{:S(2)}, u32[]{:S(2)}) collective-permute-start(bf16[256,128]{0,1:T(8,128)(2,1)S(1)} %pad_maximum_fusion.2), channel_id=1, source_target_pairs={{0,1},{1,0},{2,3},{3,2},{4,5},{5,4},{6,7},{7,6},{8,9},{9,8},{10,11... | collective-permute-start | bytes 196616 | tf_op jit(solution)/shard_map/ppermute | solution.py:37
  19.2 16.9 %copy-start.2 = (bf16[8,64,1024]{2,1,0:T(8,128)(2,1)}, bf16[8,64,1024]{2,1,0:T(8,128)(2,1)S(1)}, u32[]{:S(2)}) copy-start(bf16[8,64,1024]{2,1,0:T(8,128)(2,1)S(1)} %fusion.8) | copy-start | bytes 3145732
  19.2 24.1 %collective-permute-start.3 = (bf16[8,64,1024]{2,1,0:T(8,128)(2,1)S(1)}, bf16[8,64,1024]{2,1,0:T(8,128)(2,1)}, u32[]{:S(2)}, u32[]{:S(2)}) collective-permute-start(bf16[8,64,1024]{2,1,0:T(8,128)(2,1)S(1)} %fusion.8), channel_id=1, source_target_pairs={{0,1},{1,0},{2,3},{3,2},{4,5},{5,4},{6,7},{7,6},{8,9},{9,8},{10,11... | collective-permute-start | bytes 3145736 | tf_op jit(solution)/shard_map/ppermute | solution.py:37
  25.1 14.0 %collective-permute-start.5 = (bf16[48,1024]{1,0:T(8,128)(2,1)S(1)}, bf16[48,1024]{1,0:T(8,128)(2,1)S(1)}, u32[]{:S(2)}, u32[]{:S(2)}) collective-permute-start(bf16[48,1024]{1,0:T(8,128)(2,1)S(1)} %convolution_convert_fusion.15), channel_id=1, source_target_pairs={{2,4},{4,2},{3,5},{5,3},{6,8},{8,6},{7,9},{9,7},{10,12},{12,10},{1... | collective-permute-start | bytes 294920 | tf_op jit(solution)/shard_map/ppermute | solution.py:44
  36.1 6.9 %collective-permute-start.4 = (bf16[48,1024]{1,0:T(8,128)(2,1)S(1)}, bf16[48,1024]{1,0:T(8,128)(2,1)S(1)}, u32[]{:S(2)}, u32[]{:S(2)}) collective-permute-start(bf16[48,1024]{1,0:T(8,128)(2,1)S(1)} %convolution_convert_fusion.16), channel_id=1, source_target_pairs={{0,2},{2,0},{1,3},{3,1},{4,6},{6,4},{5,7},{7,5},{8,10},{10,8},{9,1... | collective-permute-start | bytes 294920 | tf_op jit(solution)/shard_map/ppermute | solution.py:44
  38.1 5.3 %copy-start.3 = (bf16[8,64,1024]{2,1,0:T(8,128)(2,1)S(1)}, bf16[8,64,1024]{2,1,0:T(8,128)(2,1)}, u32[]{:S(2)}) copy-start(bf16[8,64,1024]{2,1,0:T(8,128)(2,1)} %copy-done.2) | copy-start | bytes 3145732
  119.2 10.2 %collective-permute-start.7 = (bf16[48,1024]{1,0:T(8,128)(2,1)S(1)}, bf16[48,1024]{1,0:T(8,128)(2,1)S(1)}, u32[]{:S(2)}, u32[]{:S(2)}) collective-permute-start(bf16[48,1024]{1,0:T(8,128)(2,1)S(1)} %convolution_convert_fusion.13), channel_id=1, source_target_pairs={{2,4},{4,2},{3,5},{5,3},{6,8},{8,6},{7,9},{9,7},{10,12},{12,10},{1... | collective-permute-start | bytes 294920 | tf_op jit(solution)/shard_map/ppermute | solution.py:44
  123.9 6.5 %collective-permute-start.6 = (bf16[48,1024]{1,0:T(8,128)(2,1)S(1)}, bf16[48,1024]{1,0:T(8,128)(2,1)S(1)}, u32[]{:S(2)}, u32[]{:S(2)}) collective-permute-start(bf16[48,1024]{1,0:T(8,128)(2,1)S(1)} %convolution_convert_fusion.14), channel_id=1, source_target_pairs={{0,2},{2,0},{1,3},{3,1},{4,6},{6,4},{5,7},{7,5},{8,10},{10,8},{9,1... | collective-permute-start | bytes 294920 | tf_op jit(solution)/shard_map/ppermute | solution.py:44
  134.0 9.8 %collective-permute-start.9 = (bf16[48,1024]{1,0:T(8,128)(2,1)S(1)}, bf16[48,1024]{1,0:T(8,128)(2,1)S(1)}, u32[]{:S(2)}, u32[]{:S(2)}) collective-permute-start(bf16[48,1024]{1,0:T(8,128)(2,1)S(1)} %convolution_convert_fusion.11), channel_id=1, source_target_pairs={{2,4},{4,2},{3,5},{5,3},{6,8},{8,6},{7,9},{9,7},{10,12},{12,10},{1... | collective-permute-start | bytes 294920 | tf_op jit(solution)/shard_map/ppermute | solution.py:44
  139.1 6.5 %collective-permute-start.8 = (bf16[48,1024]{1,0:T(8,128)(2,1)S(1)}, bf16[48,1024]{1,0:T(8,128)(2,1)S(1)}, u32[]{:S(2)}, u32[]{:S(2)}) collective-permute-start(bf16[48,1024]{1,0:T(8,128)(2,1)S(1)} %convolution_convert_fusion.12), channel_id=1, source_target_pairs={{0,2},{2,0},{1,3},{3,1},{4,6},{6,4},{5,7},{7,5},{8,10},{10,8},{9,1... | collective-permute-start | bytes 294920 | tf_op jit(solution)/shard_map/ppermute | solution.py:44
  149.2 9.8 %collective-permute-start.11 = (bf16[48,1024]{1,0:T(8,128)(2,1)S(1)}, bf16[48,1024]{1,0:T(8,128)(2,1)S(1)}, u32[]{:S(2)}, u32[]{:S(2)}) collective-permute-start(bf16[48,1024]{1,0:T(8,128)(2,1)S(1)} %convolution_convert_fusion.9), channel_id=1, source_target_pairs={{2,4},{4,2},{3,5},{5,3},{6,8},{8,6},{7,9},{9,7},{10,12},{12,10},{1... | collective-permute-start | bytes 294920 | tf_op jit(solution)/shard_map/ppermute | solution.py:44
  153.8 6.5 %collective-permute-start.10 = (bf16[48,1024]{1,0:T(8,128)(2,1)S(1)}, bf16[48,1024]{1,0:T(8,128)(2,1)S(1)}, u32[]{:S(2)}, u32[]{:S(2)}) collective-permute-start(bf16[48,1024]{1,0:T(8,128)(2,1)S(1)} %convolution_convert_fusion.10), channel_id=1, source_target_pairs={{0,2},{2,0},{1,3},{3,1},{4,6},{6,4},{5,7},{7,5},{8,10},{10,8},{9,1... | collective-permute-start | bytes 294920 | tf_op jit(solution)/shard_map/ppermute | solution.py:44
  163.9 9.8 %collective-permute-start.13 = (bf16[48,1024]{1,0:T(8,128)(2,1)S(1)}, bf16[48,1024]{1,0:T(8,128)(2,1)S(1)}, u32[]{:S(2)}, u32[]{:S(2)}) collective-permute-start(bf16[48,1024]{1,0:T(8,128)(2,1)S(1)} %convolution_convert_fusion.7), channel_id=1, source_target_pairs={{2,4},{4,2},{3,5},{5,3},{6,8},{8,6},{7,9},{9,7},{10,12},{12,10},{1... | collective-permute-start | bytes 294920 | tf_op jit(solution)/shard_map/ppermute | solution.py:44
  169.1 6.5 %collective-permute-start.12 = (bf16[48,1024]{1,0:T(8,128)(2,1)S(1)}, bf16[48,1024]{1,0:T(8,128)(2,1)S(1)}, u32[]{:S(2)}, u32[]{:S(2)}) collective-permute-start(bf16[48,1024]{1,0:T(8,128)(2,1)S(1)} %convolution_convert_fusion.8), channel_id=1, source_target_pairs={{0,2},{2,0},{1,3},{3,1},{4,6},{6,4},{5,7},{7,5},{8,10},{10,8},{9,1... | collective-permute-start | bytes 294920 | tf_op jit(solution)/shard_map/ppermute | solution.py:44
  179.1 9.8 %collective-permute-start.15 = (bf16[48,1024]{1,0:T(8,128)(2,1)S(1)}, bf16[48,1024]{1,0:T(8,128)(2,1)S(1)}, u32[]{:S(2)}, u32[]{:S(2)}) collective-permute-start(bf16[48,1024]{1,0:T(8,128)(2,1)S(1)} %convolution_convert_fusion.5), channel_id=1, source_target_pairs={{2,4},{4,2},{3,5},{5,3},{6,8},{8,6},{7,9},{9,7},{10,12},{12,10},{1... | collective-permute-start | bytes 294920 | tf_op jit(solution)/shard_map/ppermute | solution.py:44
  183.8 6.5 %collective-permute-start.14 = (bf16[48,1024]{1,0:T(8,128)(2,1)S(1)}, bf16[48,1024]{1,0:T(8,128)(2,1)S(1)}, u32[]{:S(2)}, u32[]{:S(2)}) collective-permute-start(bf16[48,1024]{1,0:T(8,128)(2,1)S(1)} %convolution_convert_fusion.6), channel_id=1, source_target_pairs={{0,2},{2,0},{1,3},{3,1},{4,6},{6,4},{5,7},{7,5},{8,10},{10,8},{9,1... | collective-permute-start | bytes 294920 | tf_op jit(solution)/shard_map/ppermute | solution.py:44
  193.8 9.8 %collective-permute-start.17 = (bf16[48,1024]{1,0:T(8,128)(2,1)S(1)}, bf16[48,1024]{1,0:T(8,128)(2,1)S(1)}, u32[]{:S(2)}, u32[]{:S(2)}) collective-permute-start(bf16[48,1024]{1,0:T(8,128)(2,1)S(1)} %convolution_convert_fusion.3), channel_id=1, source_target_pairs={{2,4},{4,2},{3,5},{5,3},{6,8},{8,6},{7,9},{9,7},{10,12},{12,10},{1... | collective-permute-start | bytes 294920 | tf_op jit(solution)/shard_map/ppermute | solution.py:44
  199.0 6.5 %collective-permute-start.16 = (bf16[48,1024]{1,0:T(8,128)(2,1)S(1)}, bf16[48,1024]{1,0:T(8,128)(2,1)S(1)}, u32[]{:S(2)}, u32[]{:S(2)}) collective-permute-start(bf16[48,1024]{1,0:T(8,128)(2,1)S(1)} %convolution_convert_fusion.4), channel_id=1, source_target_pairs={{0,2},{2,0},{1,3},{3,1},{4,6},{6,4},{5,7},{7,5},{8,10},{10,8},{9,1... | collective-permute-start | bytes 294920 | tf_op jit(solution)/shard_map/ppermute | solution.py:44
  209.1 9.8 %collective-permute-start.19 = (bf16[48,1024]{1,0:T(8,128)(2,1)S(1)}, bf16[48,1024]{1,0:T(8,128)(2,1)S(1)}, u32[]{:S(2)}, u32[]{:S(2)}) collective-permute-start(bf16[48,1024]{1,0:T(8,128)(2,1)S(1)} %convolution_convert_fusion.1), channel_id=1, source_target_pairs={{2,4},{4,2},{3,5},{5,3},{6,8},{8,6},{7,9},{9,7},{10,12},{12,10},{1... | collective-permute-start | bytes 294920 | tf_op jit(solution)/shard_map/ppermute | solution.py:44
  213.7 6.5 %collective-permute-start.18 = (bf16[48,1024]{1,0:T(8,128)(2,1)S(1)}, bf16[48,1024]{1,0:T(8,128)(2,1)S(1)}, u32[]{:S(2)}, u32[]{:S(2)}) collective-permute-start(bf16[48,1024]{1,0:T(8,128)(2,1)S(1)} %convolution_convert_fusion.2), channel_id=1, source_target_pairs={{0,2},{2,0},{1,3},{3,1},{4,6},{6,4},{5,7},{7,5},{8,10},{10,8},{9,1... | collective-permute-start | bytes 294920 | tf_op jit(solution)/shard_map/ppermute | solution.py:44
  244.4 1.5 copy-start.1
Sparse Core Ops, SparseCore 0:
  10.6 104.6 all-gather.1
where the time goes:
time: 254 us; the launch traced here: 253 us
  waiting for transfers between devices  104 us (41%)
  starting transfers between devices  66.9 us (26%)
  matrix products  35.9 us (14%)
  blocking collectives  21.4 us (8%)
  between operations  14.1 us (6%)
  local copies, waits for them, and re-layouts  7.57 us (3%)
  other arithmetic  3.38 us (1%)
    all_gather x1, waiting for transfers between devices, shards(): resident = lax.all_gather(weights, 'graph', axis=1, tiled=True)  68.9 us
    ppermute x16, starting transfers between devices, exchange(): return lax.ppermute(value, 'graph', pairs)  58.2 us
    ppermute x16, waiting for transfers between devices, exchange(): return lax.ppermute(value, 'graph', pairs)  34 us
    dot_general x33, matrix products, dot(): return jnp.dot(a, b, preferred_element_type=F32)  27.5 us
    all_to_all x1, blocking collectives, shards(): exchanged = lax.all_to_all(whole, 'segment', 0, 0)  21.4 us
    ppermute x4, starting transfers between devices, partner(): lax.ppermute(value, 'graph', [(p, p ^ 1) for p in range(graph_count)])  8.64 us
    dot_general x26, matrix products, dot_t(): lax.dot_general(a, b, (((0,), (0,)), ((), ())), preferred_element_type=F32)  8.4 us
  transfers between devices with their start and end apart: 21, of which 17 were waited for; matrix products, arithmetic and copies ran while one was open for 7% of the time, Pallas kernels for 0%

commit v1 on v0

--- a/solution.py
+++ b/solution.py
@@ -1,3 +1,4 @@
+import functools
 import jax
 import jax.numpy as jnp
 from jax import lax
@@ -7,6 +8,15 @@
 LAMBDA = 1.5
 BF = jnp.bfloat16
 F32 = jnp.float32
+
+
+def launch_digits_on_mesh(local_x, dim_k):
+    vec_out = jnp.stack([local_x] * lax.axis_size("graph"))
+    x_next = lax.all_to_all(vec_out, axis_name="graph", split_axis=0, concat_axis=0)
+    return jnp.concatenate(x_next, axis=dim_k)
+
+
+list_the_lane = functools.partial(launch_digits_on_mesh, dim_k=1)
 
 
 def dot(a, b):
@@ -31,7 +41,7 @@
     rows = own_adj.shape[2]
     edge = send_ids.shape[2]
     kept = layers // segment_count
-    resident = lax.all_gather(weights, "graph", axis=1, tiled=True)
+    resident = list_the_lane(weights)
 
     def partner(value):
         return lax.ppermute(value, "graph", [(p, p ^ 1) for p in range(graph_count)])

time: 254 us -> 690 us (2.72)
  waiting for transfers between devices: 104 us -> 513 us
  starting transfers between devices: 66.9 us -> 99.4 us
  between operations: 14.1 us -> 0.8 us
    ppermute x16, waiting for transfers between devices: 34 us -> 344 us  [exchange(): return lax.ppermute(value, 'graph', pairs)]
    all_to_all x0 -> x1, waiting for transfers between devices: none -> 169 us  [launch_digits_on_mesh(): lax.all_to_all(vec_out, axis_name='graph', split_axis=0, concat_axis=0)]
    all_gather x1 -> x0, waiting for transfers between devices: 68.9 us -> none  [shards(): resident = lax.all_gather(weights, 'graph', axis=1, tiled=True)]
    all_to_all x0 -> x1, starting transfers between devices: none -> 17.9 us  [launch_digits_on_mesh(): lax.all_to_all(vec_out, axis_name='graph', split_axis=0, concat_axis=0)]
    ppermute x16, starting transfers between devices: 58.2 us -> 72.9 us  [exchange(): return lax.ppermute(value, 'graph', pairs)]
  transfers between devices with their start and end apart: 21 -> 21, of which waited for: 17 -> 10; matrix products, arithmetic and copies ran while one was open for 7% -> 3% of each run, Pallas kernels for 0% -> 0%
where the time goes in v1:
time: 690 us; the launch traced here: 689 us
  waiting for transfers between devices  513 us (74%)
  starting transfers between devices  99.4 us (14%)
  matrix products  35.9 us (5%)
  blocking collectives  22.3 us (3%)
  local copies, waits for them, and re-layouts  14.2 us (2%)
    ppermute x16, waiting for transfers between devices, exchange(): return lax.ppermute(value, 'graph', pairs)  344 us
    all_to_all x1, waiting for transfers between devices, launch_digits_on_mesh(): lax.all_to_all(vec_out, axis_name='graph', split_axis=0, concat_axis=0)  169 us
    ppermute x16, starting transfers between devices, exchange(): return lax.ppermute(value, 'graph', pairs)  72.9 us
    dot_general x33, matrix products, dot(): return jnp.dot(a, b, preferred_element_type=F32)  27.4 us
    all_to_all x1, blocking collectives, shards(): exchanged = lax.all_to_all(whole, 'segment', 0, 0)  22.3 us
    all_to_all x1, starting transfers between devices, launch_digits_on_mesh(): lax.all_to_all(vec_out, axis_name='graph', split_axis=0, concat_axis=0)  17.9 us
  transfers between devices with their start and end apart: 21, of which 10 were waited for; matrix products, arithmetic and copies ran while one was open for 3% of the time, Pallas kernels for 0%

profile of v1, /device:TPU:32, one launch (start us, length us, event | category | flops | bytes accessed | tf_op | source)
XLA Modules:
  0.0 689.0 jit_solution(9694991521052842440)
XLA Ops:
  0.0 6.9 stack.20
  6.9 17.9 %all-to-all-start = ((bf16[128,8,8,1024]{3,2,1,0:T(8,128)(2,1)}), bf16[128,8,8,1024]{3,2,1,0:T(8,128)(2,1)}, u32[]{:S(2)}, u32[]{:S(2)}) async-start(bf16[128,8,8,1024]{3,2,1,0:T(8,128)(2,1)} %stack.20), calls=%async_computation | async-start | bytes 33554432 | tf_op jit(solution)/shard_map/all_to_all | solution.py:15
  31.7 2.3 collective-permute-start
  37.2 2.3 collective-permute-start.3
  42.9 3.4 collective-permute-start.4
  46.5 4.5 collective-permute-start.5
  51.0 284.1 %collective-permute-done.4 = bf16[48,1024]{1,0:T(8,128)(2,1)S(1)} collective-permute-done((bf16[48,1024]{1,0:T(8,128)(2,1)S(1)}, bf16[48,1024]{1,0:T(8,128)(2,1)S(1)}, u32[]{:S(2)}, u32[]{:S(2)}) %collective-permute-start.4) | collective-permute-done | bytes 98336 | tf_op jit(solution)/shard_map/ppermute | solution.py:54
  335.4 7.8 %collective-permute-done.5 = bf16[48,1024]{1,0:T(8,128)(2,1)S(1)} collective-permute-done((bf16[48,1024]{1,0:T(8,128)(2,1)S(1)}, bf16[48,1024]{1,0:T(8,128)(2,1)S(1)}, u32[]{:S(2)}, u32[]{:S(2)}) %collective-permute-start.5) | collective-permute-done | bytes 98336 | tf_op jit(solution)/shard_map/ppermute | solution.py:54
  346.6 168.8 %all-to-all-done = bf16[128,8,8,1024]{3,2,1,0:T(8,128)(2,1)} async-done(((bf16[128,8,8,1024]{3,2,1,0:T(8,128)(2,1)}), bf16[128,8,8,1024]{3,2,1,0:T(8,128)(2,1)}, u32[]{:S(2)}, u32[]{:S(2)}) %all-to-all-start) | async-done | bytes 16777248 | tf_op jit(solution)/shard_map/all_to_all | solution.py:15
  515.5 3.0 maximum_convert_fusion.6
  519.3 38.9 %collective-permute-start.6 = (bf16[48,1024]{1,0:T(8,128)(2,1)S(1)}, bf16[48,1024]{1,0:T(8,128)(2,1)S(1)}, u32[]{:S(2)}, u32[]{:S(2)}) collective-permute-start(bf16[48,1024]{1,0:T(8,128)(2,1)S(1)} %convolution_convert_fusion.14), channel_id=1, source_target_pairs={{0,2},{2,0},{1,3},{3,1},{4,6},{6,4},{5,7},{7,5},{8,10},{10,8},{9,1... | collective-permute-start | bytes 294920 | tf_op jit(solution)/shard_map/ppermute | solution.py:54
  560.5 7.6 %collective-permute-done.7 = bf16[48,1024]{1,0:T(8,128)(2,1)S(1)} collective-permute-done((bf16[48,1024]{1,0:T(8,128)(2,1)S(1)}, bf16[48,1024]{1,0:T(8,128)(2,1)S(1)}, u32[]{:S(2)}, u32[]{:S(2)}) %collective-permute-start.7) | collective-permute-done | bytes 98336 | tf_op jit(solution)/shard_map/ppermute | solution.py:54
  568.8 2.4 maximum_convert_fusion.5
  573.9 2.1 collective-permute-start.9
  576.3 7.4 %collective-permute-done.9 = bf16[48,1024]{1,0:T(8,128)(2,1)S(1)} collective-permute-done((bf16[48,1024]{1,0:T(8,128)(2,1)S(1)}, bf16[48,1024]{1,0:T(8,128)(2,1)S(1)}, u32[]{:S(2)}, u32[]{:S(2)}) %collective-permute-start.9) | collective-permute-done | bytes 98336 | tf_op jit(solution)/shard_map/ppermute | solution.py:54
  584.4 2.4 maximum_convert_fusion.4
  589.5 2.1 collective-permute-start.11
  591.9 7.4 %collective-permute-done.11 = bf16[48,1024]{1,0:T(8,128)(2,1)S(1)} collective-permute-done((bf16[48,1024]{1,0:T(8,128)(2,1)S(1)}, bf16[48,1024]{1,0:T(8,128)(2,1)S(1)}, u32[]{:S(2)}, u32[]{:S(2)}) %collective-permute-start.11) | collective-permute-done | bytes 98336 | tf_op jit(solution)/shard_map/ppermute | solution.py:54
  600.1 2.4 maximum_convert_fusion.3
  605.2 2.2 collective-permute-start.13
  607.8 7.2 %collective-permute-done.13 = bf16[48,1024]{1,0:T(8,128)(2,1)S(1)} collective-permute-done((bf16[48,1024]{1,0:T(8,128)(2,1)S(1)}, bf16[48,1024]{1,0:T(8,128)(2,1)S(1)}, u32[]{:S(2)}, u32[]{:S(2)}) %collective-permute-start.13) | collective-permute-done | bytes 98336 | tf_op jit(solution)/shard_map/ppermute | solution.py:54
  615.7 2.4 maximum_convert_fusion.2
  620.9 2.1 collective-permute-start.15
  623.3 7.4 %collective-permute-done.15 = bf16[48,1024]{1,0:T(8,128)(2,1)S(1)} collective-permute-done((bf16[48,1024]{1,0:T(8,128)(2,1)S(1)}, bf16[48,1024]{1,0:T(8,128)(2,1)S(1)}, u32[]{:S(2)}, u32[]{:S(2)}) %collective-permute-start.15) | collective-permute-done | bytes 98336 | tf_op jit(solution)/shard_map/ppermute | solution.py:54
  631.4 2.4 maximum_convert_fusion.1
  636.5 2.1 collective-permute-start.17
  638.9 7.4 %collective-permute-done.17 = bf16[48,1024]{1,0:T(8,128)(2,1)S(1)} collective-permute-done((bf16[48,1024]{1,0:T(8,128)(2,1)S(1)}, bf16[48,1024]{1,0:T(8,128)(2,1)S(1)}, u32[]{:S(2)}, u32[]{:S(2)}) %collective-permute-start.17) | collective-permute-done | bytes 98336 | tf_op jit(solution)/shard_map/ppermute | solution.py:54
  647.1 2.4 maximum_convert_fusion
  652.2 2.1 collective-permute-start.19
  654.6 7.4 %collective-permute-done.19 = bf16[48,1024]{1,0:T(8,128)(2,1)S(1)} collective-permute-done((bf16[48,1024]{1,0:T(8,128)(2,1)S(1)}, bf16[48,1024]{1,0:T(8,128)(2,1)S(1)}, u32[]{:S(2)}, u32[]{:S(2)}) %collective-permute-start.19) | collective-permute-done | bytes 98336 | tf_op jit(solution)/shard_map/ppermute | solution.py:54
  662.7 2.3 fusion
  665.2 22.3 %all_to_all.10 = bf16[4,2,128,1024]{3,2,1,0:T(8,128)(2,1)S(1)} all-to-all(bf16[4,2,128,1024]{3,2,1,0:T(8,128)(2,1)S(1)} %bitcast.147), channel_id=1, replica_groups=mesh['segment'=4,'graph'=128] {'segment'}, dimensions={0} | all-to-all | bytes 4194304 | tf_op jit(solution)/shard_map/all_to_all | solution.py:144
  (125 shorter events, 44.7 us)
Async XLA Ops:
  0.0 36.7 %copy-start = (bf16[8,64,1024]{2,1,0:T(8,128)(2,1)S(1)}, bf16[8,64,1024]{2,1,0:T(8,128)(2,1)}, u32[]{:S(2)}) copy-start(bf16[8,64,1024]{2,1,0:T(8,128)(2,1)} %param.10) | copy-start | bytes 3145732
  6.9 27.1 %copy-start.4 = (bf16[512,1024]{1,0:T(8,128)(2,1)S(1)}, bf16[512,1024]{1,0:T(8,128)(2,1)}, u32[]{:S(2)}) copy-start(bf16[512,1024]{1,0:T(8,128)(2,1)} %param.8) | copy-start | bytes 3145732
  6.9 508.6 %all-to-all-start = ((bf16[128,8,8,1024]{3,2,1,0:T(8,128)(2,1)}), bf16[128,8,8,1024]{3,2,1,0:T(8,128)(2,1)}, u32[]{:S(2)}, u32[]{:S(2)}) async-start(bf16[128,8,8,1024]{3,2,1,0:T(8,128)(2,1)} %stack.20), calls=%async_computation | async-start | bytes 33554432 | tf_op jit(solution)/shard_map/all_to_all | solution.py:15
  26.4 13.2 %collective-permute-start.1 = (s32[128]{0:T(128)S(1)}, s32[128]{0:T(128)S(1)}, u32[]{:S(2)}, u32[]{:S(2)}) collective-permute-start(s32[128]{0:T(128)S(1)} %pad_add_fusion.4), channel_id=1, source_target_pairs={{0,1},{1,0},{2,3},{3,2},{4,5},{5,4},{6,7},{7,6},{8,9},{9,8},{10,11... | collective-permute-start | bytes 1544 | tf_op jit(solution)/shard_map/ppermute | solution.py:47
  31.7 8.5 %collective-permute-start = (bf16[256,128]{0,1:T(8,128)(2,1)}, bf16[256,128]{0,1:T(8,128)(2,1)}, u32[]{:S(2)}, u32[]{:S(2)}) collective-permute-start(bf16[256,128]{0,1:T(8,128)(2,1)} %pad_maximum_fusion.2), channel_id=1, source_target_pairs={{0,1},{1,0},{2,3},{3,2},{4,5},{5,4},{6,7},{7,6},{8,9},{9,8},{10,11... | collective-permute-start | bytes 196616 | tf_op jit(solution)/shard_map/ppermute | solution.py:47
  34.7 7.8 %collective-permute-start.2 = (bf16[128,1024]{1,0:T(8,128)(2,1)}, bf16[128,1024]{1,0:T(8,128)(2,1)S(1)}, u32[]{:S(2)}, u32[]{:S(2)}) collective-permute-start(bf16[128,1024]{1,0:T(8,128)(2,1)} %constant_dynamic-slice_fusion), channel_id=1, source_target_pairs={{0,1},{1,0},{2,3},{3,2},{4,5},{5,4},{6,7},{7,6},{8,9},{9,8},{10,11... | collective-permute-start | bytes 786440 | tf_op jit(solution)/shard_map/ppermute | solution.py:47
  37.2 9.2 %copy-start.2 = (bf16[8,64,1024]{2,1,0:T(8,128)(2,1)}, bf16[8,64,1024]{2,1,0:T(8,128)(2,1)S(1)}, u32[]{:S(2)}) copy-start(bf16[8,64,1024]{2,1,0:T(8,128)(2,1)S(1)} %fusion.8) | copy-start | bytes 3145732
  37.2 306.3 %collective-permute-start.3 = (bf16[8,64,1024]{2,1,0:T(8,128)(2,1)S(1)}, bf16[8,64,1024]{2,1,0:T(8,128)(2,1)}, u32[]{:S(2)}, u32[]{:S(2)}) collective-permute-start(bf16[8,64,1024]{2,1,0:T(8,128)(2,1)S(1)} %fusion.8), channel_id=1, source_target_pairs={{0,1},{1,0},{2,3},{3,2},{4,5},{5,4},{6,7},{7,6},{8,9},{9,8},{10,11... | collective-permute-start | bytes 3145736 | tf_op jit(solution)/shard_map/ppermute | solution.py:47
  42.9 292.2 %collective-permute-start.4 = (bf16[48,1024]{1,0:T(8,128)(2,1)S(1)}, bf16[48,1024]{1,0:T(8,128)(2,1)S(1)}, u32[]{:S(2)}, u32[]{:S(2)}) collective-permute-start(bf16[48,1024]{1,0:T(8,128)(2,1)S(1)} %convolution_convert_fusion.16), channel_id=1, source_target_pairs={{0,2},{2,0},{1,3},{3,1},{4,6},{6,4},{5,7},{7,5},{8,10},{10,8},{9,1... | collective-permute-start | bytes 294920 | tf_op jit(solution)/shard_map/ppermute | solution.py:54
  46.5 296.7 %collective-permute-start.5 = (bf16[48,1024]{1,0:T(8,128)(2,1)S(1)}, bf16[48,1024]{1,0:T(8,128)(2,1)S(1)}, u32[]{:S(2)}, u32[]{:S(2)}) collective-permute-start(bf16[48,1024]{1,0:T(8,128)(2,1)S(1)} %convolution_convert_fusion.15), channel_id=1, source_target_pairs={{2,4},{4,2},{3,5},{5,3},{6,8},{8,6},{7,9},{9,7},{10,12},{12,10},{1... | collective-permute-start | bytes 294920 | tf_op jit(solution)/shard_map/ppermute | solution.py:54
  51.0 292.5 %copy-start.3 = (bf16[8,64,1024]{2,1,0:T(8,128)(2,1)S(1)}, bf16[8,64,1024]{2,1,0:T(8,128)(2,1)}, u32[]{:S(2)}) copy-start(bf16[8,64,1024]{2,1,0:T(8,128)(2,1)} %copy-done.2) | copy-start | bytes 3145732
  519.3 49.1 %collective-permute-start.6 = (bf16[48,1024]{1,0:T(8,128)(2,1)S(1)}, bf16[48,1024]{1,0:T(8,128)(2,1)S(1)}, u32[]{:S(2)}, u32[]{:S(2)}) collective-permute-start(bf16[48,1024]{1,0:T(8,128)(2,1)S(1)} %convolution_convert_fusion.14), channel_id=1, source_target_pairs={{0,2},{2,0},{1,3},{3,1},{4,6},{6,4},{5,7},{7,5},{8,10},{10,8},{9,1... | collective-permute-start | bytes 294920 | tf_op jit(solution)/shard_map/ppermute | solution.py:54
  558.2 9.8 %collective-permute-start.7 = (bf16[48,1024]{1,0:T(8,128)(2,1)S(1)}, bf16[48,1024]{1,0:T(8,128)(2,1)S(1)}, u32[]{:S(2)}, u32[]{:S(2)}) collective-permute-start(bf16[48,1024]{1,0:T(8,128)(2,1)S(1)} %convolution_convert_fusion.13), channel_id=1, source_target_pairs={{2,4},{4,2},{3,5},{5,3},{6,8},{8,6},{7,9},{9,7},{10,12},{12,10},{1... | collective-permute-start | bytes 294920 | tf_op jit(solution)/shard_map/ppermute | solution.py:54
  571.9 12.1 %collective-permute-start.8 = (bf16[48,1024]{1,0:T(8,128)(2,1)S(1)}, bf16[48,1024]{1,0:T(8,128)(2,1)S(1)}, u32[]{:S(2)}, u32[]{:S(2)}) collective-permute-start(bf16[48,1024]{1,0:T(8,128)(2,1)S(1)} %convolution_convert_fusion.12), channel_id=1, source_target_pairs={{0,2},{2,0},{1,3},{3,1},{4,6},{6,4},{5,7},{7,5},{8,10},{10,8},{9,1... | collective-permute-start | bytes 294920 | tf_op jit(solution)/shard_map/ppermute | solution.py:54
  573.9 9.8 %collective-permute-start.9 = (bf16[48,1024]{1,0:T(8,128)(2,1)S(1)}, bf16[48,1024]{1,0:T(8,128)(2,1)S(1)}, u32[]{:S(2)}, u32[]{:S(2)}) collective-permute-start(bf16[48,1024]{1,0:T(8,128)(2,1)S(1)} %convolution_convert_fusion.11), channel_id=1, source_target_pairs={{2,4},{4,2},{3,5},{5,3},{6,8},{8,6},{7,9},{9,7},{10,12},{12,10},{1... | collective-permute-start | bytes 294920 | tf_op jit(solution)/shard_map/ppermute | solution.py:54
  587.6 12.1 %collective-permute-start.10 = (bf16[48,1024]{1,0:T(8,128)(2,1)S(1)}, bf16[48,1024]{1,0:T(8,128)(2,1)S(1)}, u32[]{:S(2)}, u32[]{:S(2)}) collective-permute-start(bf16[48,1024]{1,0:T(8,128)(2,1)S(1)} %convolution_convert_fusion.10), channel_id=1, source_target_pairs={{0,2},{2,0},{1,3},{3,1},{4,6},{6,4},{5,7},{7,5},{8,10},{10,8},{9,1... | collective-permute-start | bytes 294920 | tf_op jit(solution)/shard_map/ppermute | solution.py:54
  589.5 9.8 %collective-permute-start.11 = (bf16[48,1024]{1,0:T(8,128)(2,1)S(1)}, bf16[48,1024]{1,0:T(8,128)(2,1)S(1)}, u32[]{:S(2)}, u32[]{:S(2)}) collective-permute-start(bf16[48,1024]{1,0:T(8,128)(2,1)S(1)} %convolution_convert_fusion.9), channel_id=1, source_target_pairs={{2,4},{4,2},{3,5},{5,3},{6,8},{8,6},{7,9},{9,7},{10,12},{12,10},{1... | collective-permute-start | bytes 294920 | tf_op jit(solution)/shard_map/ppermute | solution.py:54
  603.3 12.1 %collective-permute-start.12 = (bf16[48,1024]{1,0:T(8,128)(2,1)S(1)}, bf16[48,1024]{1,0:T(8,128)(2,1)S(1)}, u32[]{:S(2)}, u32[]{:S(2)}) collective-permute-start(bf16[48,1024]{1,0:T(8,128)(2,1)S(1)} %convolution_convert_fusion.8), channel_id=1, source_target_pairs={{0,2},{2,0},{1,3},{3,1},{4,6},{6,4},{5,7},{7,5},{8,10},{10,8},{9,1... | collective-permute-start | bytes 294920 | tf_op jit(solution)/shard_map/ppermute | solution.py:54
  605.2 9.8 %collective-permute-start.13 = (bf16[48,1024]{1,0:T(8,128)(2,1)S(1)}, bf16[48,1024]{1,0:T(8,128)(2,1)S(1)}, u32[]{:S(2)}, u32[]{:S(2)}) collective-permute-start(bf16[48,1024]{1,0:T(8,128)(2,1)S(1)} %convolution_convert_fusion.7), channel_id=1, source_target_pairs={{2,4},{4,2},{3,5},{5,3},{6,8},{8,6},{7,9},{9,7},{10,12},{12,10},{1... | collective-permute-start | bytes 294920 | tf_op jit(solution)/shard_map/ppermute | solution.py:54
  618.9 12.1 %collective-permute-start.14 = (bf16[48,1024]{1,0:T(8,128)(2,1)S(1)}, bf16[48,1024]{1,0:T(8,128)(2,1)S(1)}, u32[]{:S(2)}, u32[]{:S(2)}) collective-permute-start(bf16[48,1024]{1,0:T(8,128)(2,1)S(1)} %convolution_convert_fusion.6), channel_id=1, source_target_pairs={{0,2},{2,0},{1,3},{3,1},{4,6},{6,4},{5,7},{7,5},{8,10},{10,8},{9,1... | collective-permute-start | bytes 294920 | tf_op jit(solution)/shard_map/ppermute | solution.py:54
  620.9 9.8 %collective-permute-start.15 = (bf16[48,1024]{1,0:T(8,128)(2,1)S(1)}, bf16[48,1024]{1,0:T(8,128)(2,1)S(1)}, u32[]{:S(2)}, u32[]{:S(2)}) collective-permute-start(bf16[48,1024]{1,0:T(8,128)(2,1)S(1)} %convolution_convert_fusion.5), channel_id=1, source_target_pairs={{2,4},{4,2},{3,5},{5,3},{6,8},{8,6},{7,9},{9,7},{10,12},{12,10},{1... | collective-permute-start | bytes 294920 | tf_op jit(solution)/shard_map/ppermute | solution.py:54
  634.6 12.1 %collective-permute-start.16 = (bf16[48,1024]{1,0:T(8,128)(2,1)S(1)}, bf16[48,1024]{1,0:T(8,128)(2,1)S(1)}, u32[]{:S(2)}, u32[]{:S(2)}) collective-permute-start(bf16[48,1024]{1,0:T(8,128)(2,1)S(1)} %convolution_convert_fusion.4), channel_id=1, source_target_pairs={{0,2},{2,0},{1,3},{3,1},{4,6},{6,4},{5,7},{7,5},{8,10},{10,8},{9,1... | collective-permute-start | bytes 294920 | tf_op jit(solution)/shard_map/ppermute | solution.py:54
  636.5 9.8 %collective-permute-start.17 = (bf16[48,1024]{1,0:T(8,128)(2,1)S(1)}, bf16[48,1024]{1,0:T(8,128)(2,1)S(1)}, u32[]{:S(2)}, u32[]{:S(2)}) collective-permute-start(bf16[48,1024]{1,0:T(8,128)(2,1)S(1)} %convolution_convert_fusion.3), channel_id=1, source_target_pairs={{2,4},{4,2},{3,5},{5,3},{6,8},{8,6},{7,9},{9,7},{10,12},{12,10},{1... | collective-permute-start | bytes 294920 | tf_op jit(solution)/shard_map/ppermute | solution.py:54
  650.3 12.1 %collective-permute-start.18 = (bf16[48,1024]{1,0:T(8,128)(2,1)S(1)}, bf16[48,1024]{1,0:T(8,128)(2,1)S(1)}, u32[]{:S(2)}, u32[]{:S(2)}) collective-permute-start(bf16[48,1024]{1,0:T(8,128)(2,1)S(1)} %convolution_convert_fusion.2), channel_id=1, source_target_pairs={{0,2},{2,0},{1,3},{3,1},{4,6},{6,4},{5,7},{7,5},{8,10},{10,8},{9,1... | collective-permute-start | bytes 294920 | tf_op jit(solution)/shard_map/ppermute | solution.py:54
  652.2 9.8 %collective-permute-start.19 = (bf16[48,1024]{1,0:T(8,128)(2,1)S(1)}, bf16[48,1024]{1,0:T(8,128)(2,1)S(1)}, u32[]{:S(2)}, u32[]{:S(2)}) collective-permute-start(bf16[48,1024]{1,0:T(8,128)(2,1)S(1)} %convolution_convert_fusion.1), channel_id=1, source_target_pairs={{2,4},{4,2},{3,5},{5,3},{6,8},{8,6},{7,9},{9,7},{10,12},{12,10},{1... | collective-permute-start | bytes 294920 | tf_op jit(solution)/shard_map/ppermute | solution.py:54
  687.5 1.5 copy-start.1
